TPU v7x, 512 devices: a whole 4x4x16 slice. The times are simulated.
512 devices in a mesh: seq: 64 (over z_lo, y, core), dp: 8 (over z_hi, x).
Axes of the slice: x: 4, y: 4, z: 16 (z_hi: 2, z_lo: 8; z = z_hi * 8 + z_lo), core: 2. Of those that a mesh axis runs over, the one named last changes fastest.
Arguments:
- q_raw: bfloat16 [8, 16384, 1024], P('dp', 'seq'), may hold values from -400 to 400
- k_raw: bfloat16 [8, 16384, 512], P('dp', 'seq'), may hold values from -400 to 400
- values: bfloat16 [8, 16384, 512], P('dp', 'seq'), may hold values from -6 to 6
- grad_out: bfloat16 [8, 16384, 1024], P('dp', 'seq'), may hold values from -80 to 80
- q_gain: float32 [256], replicated, may hold values from 0.5 to 7
- k_gain: float32 [256], replicated, may hold values from 0.5 to 7
Outputs:
- grad_q_raw: bfloat16 [8, 16384, 1024], P('dp', 'seq')
- grad_k_raw: bfloat16 [8, 16384, 512], P('dp', 'seq')
- grad_values: bfloat16 [8, 16384, 512], P('dp', 'seq')
- grad_q_gain: float32 [256], replicated
- grad_k_gain: float32 [256], replicated
All inputs are finite; a program needn't handle non-finite values.
Results may differ from a plain program's by a relative error of at most 0.029.
The roundings to bfloat16 on the way count: a program that leaves them out, or rounds other values in their place, can miss the bound.
Values may be sent and summed in bfloat16 or wider, within the bound.
A program may use at most 128 MiB of HBM per device.

v0:
```python
import jax
import jax.numpy as jnp
from jax import lax
from jax.sharding import PartitionSpec as P

WINDOW = 1024
EPS = 1e-06
ROPE_BASE = 10000.0
MASKED = -1e30


def from_behind(array, axis, by):
    count = lax.axis_size(axis)
    pairs = [(i, i + by) for i in range(count) if 0 <= i + by < count]
    return lax.ppermute(array, axis, pairs)


def rope_tables(positions, head_size):
    half_size = head_size // 2
    freqs = jnp.power(ROPE_BASE, -(2.0 * jnp.arange(half_size, dtype=jnp.float32)) / head_size)
    angles = positions.astype(jnp.float32)[:, None] * freqs[None, :]
    return (jnp.cos(angles), jnp.sin(angles))


def norm_rope(raw_in, gain_in, cosine, sine, head_count):
    head_size = gain_in.shape[0]
    row_count = raw_in.shape[0]
    inputs = raw_in.reshape(row_count, head_count, head_size)
    inverse = lax.rsqrt(jnp.mean(inputs * inputs, axis=-1, keepdims=True) + EPS)
    scaled = inputs * inverse * gain_in
    half_size = head_size // 2
    lower = scaled[..., :half_size]
    upper = scaled[..., half_size:]
    cos_rows = cosine[:, None, :]
    sin_rows = sine[:, None, :]
    turned = jnp.concatenate(
        [lower * cos_rows - upper * sin_rows, upper * cos_rows + lower * sin_rows], axis=-1
    )
    return turned.reshape(row_count, head_count * head_size)


def local(q_raw, k_raw, values, grad_out, q_gain, k_gain):
    q_local = q_raw[0]
    k_local = k_raw[0]
    v_local = values[0]
    do_local = grad_out[0]
    rows_here = q_local.shape[0]
    head_size = q_gain.shape[0]
    query_heads = q_local.shape[1] // head_size
    pair_heads = k_local.shape[1] // head_size
    group_size = query_heads // pair_heads
    reach_dev = WINDOW // rows_here
    key_span = WINDOW + rows_here
    score_scale = head_size ** (-0.5)
    first_pos = lax.axis_index("seq") * rows_here
    positions = first_pos + jnp.arange(rows_here, dtype=jnp.int32)
    cosine, sine = rope_tables(positions, head_size)
    q_rot32, q_back = jax.vjp(
        lambda raw_in, gain_in: norm_rope(raw_in, gain_in, cosine, sine, query_heads),
        q_local.astype(jnp.float32),
        q_gain,
    )
    k_rot32, k_back = jax.vjp(
        lambda raw_in, gain_in: norm_rope(raw_in, gain_in, cosine, sine, pair_heads),
        k_local.astype(jnp.float32),
        k_gain,
    )
    q_rot = q_rot32.astype(jnp.bfloat16)
    k_rot = k_rot32.astype(jnp.bfloat16)
    halo_k = []
    halo_v = []
    for offset in range(reach_dev, 0, -1):
        received = from_behind((k_rot, v_local), "seq", offset)
        halo_k.append(received[0])
        halo_v.append(received[1])
    key_rows = jnp.concatenate(halo_k + [k_rot], axis=0)
    value_rows = jnp.concatenate(halo_v + [v_local], axis=0)
    q_heads = q_rot.reshape(rows_here, pair_heads, group_size, head_size)
    k_heads = key_rows.reshape(key_span, pair_heads, head_size)
    v_heads = value_rows.reshape(key_span, pair_heads, head_size)
    do_heads = do_local.reshape(rows_here, pair_heads, group_size, head_size)
    query_idx = jnp.arange(rows_here, dtype=jnp.int32)[:, None]
    key_idx = jnp.arange(key_span, dtype=jnp.int32)[None, :]
    distance = query_idx + WINDOW - key_idx
    visible = (distance >= 0) & (distance < WINDOW) & (key_idx >= WINDOW - first_pos)
    scores = (
        jnp.einsum("tkgd,skd->kgts", q_heads, k_heads, preferred_element_type=jnp.float32)
        * score_scale
    )
    scores = jnp.where(visible, scores, MASKED)
    row_top = jnp.max(scores, axis=-1, keepdims=True)
    row_total = jnp.log(jnp.sum(jnp.exp(scores - row_top), axis=-1, keepdims=True)) + row_top
    weights = jnp.exp(scores - row_total)
    weights_b = weights.astype(jnp.bfloat16)
    dweights = jnp.einsum("tkgd,skd->kgts", do_heads, v_heads, preferred_element_type=jnp.float32)
    row_delta = jnp.sum(weights * dweights, axis=-1, keepdims=True)
    dscores = (weights * (dweights - row_delta) * score_scale).astype(jnp.bfloat16)
    dq_rot = jnp.einsum(
        "kgts,skd->tkgd", dscores, k_heads, preferred_element_type=jnp.float32
    ).reshape(rows_here, query_heads * head_size)
    dk_all = jnp.einsum("kgts,tkgd->skd", dscores, q_heads, preferred_element_type=jnp.float32)
    dv_all = jnp.einsum("kgts,tkgd->skd", weights_b, do_heads, preferred_element_type=jnp.float32)
    dk_own = dk_all[WINDOW:]
    dv_own = dv_all[WINDOW:]
    for offset in range(1, reach_dev + 1):
        low_row = (reach_dev - offset) * rows_here
        sent_k = dk_all[low_row : low_row + rows_here].astype(jnp.bfloat16)
        sent_v = dv_all[low_row : low_row + rows_here].astype(jnp.bfloat16)
        received = from_behind((sent_k, sent_v), "seq", -offset)
        dk_own = dk_own + received[0].astype(jnp.float32)
        dv_own = dv_own + received[1].astype(jnp.float32)
    dk_rot = dk_own.reshape(rows_here, pair_heads * head_size)
    grad_q_local, gain_q_local = q_back(dq_rot)
    grad_k_local, gain_k_local = k_back(dk_rot)
    gain_q_all, gain_k_all = lax.psum((gain_q_local, gain_k_local), ("seq", "dp"))
    grad_v_local = dv_own.reshape(rows_here, pair_heads * head_size).astype(jnp.bfloat16)
    return (
        grad_q_local.astype(jnp.bfloat16)[None],
        grad_k_local.astype(jnp.bfloat16)[None],
        grad_v_local[None],
        gain_q_all,
        gain_k_all,
    )


def solution(mesh):
    return jax.shard_map(
        local,
        mesh=mesh,
        in_specs=(
            P("dp", "seq", None),
            P("dp", "seq", None),
            P("dp", "seq", None),
            P("dp", "seq", None),
            P(),
            P(),
        ),
        out_specs=(P("dp", "seq", None), P("dp", "seq", None), P("dp", "seq", None), P(), P()),
        check_vma=False,
    )
```

profile of v0, /device:TPU:1, one launch (start us, length us, event | category | flops | bytes accessed | tf_op | source)
XLA Modules:
  0.0 258.1 jit_solution(8285778720912913618)
XLA Ops:
  3.4 6.4 %collective-permute-start = (bf16[256,512]{0,1:T(8,128)(2,1)S(1)}, bf16[256,512]{0,1:T(8,128)(2,1)}, u32[]{:S(2)}, u32[]{:S(2)}) collective-permute-start(bf16[256,512]{0,1:T(8,128)(2,1)S(1)} %bitcast.80), channel_id=1, source_target_pairs={{0,32},{8,40},{16,48},{24,56},{32,64},{40,72},{48,80},{56,88},{64,... | collective-permute-start | bytes 786440 | tf_op jit(solution)/shard_map/ppermute | solution.py:15
  9.7 4.2 %collective-permute-start.1 = (bf16[256,512]{0,1:T(8,128)(2,1)S(1)}, bf16[256,512]{0,1:T(8,128)(2,1)}, u32[]{:S(2)}, u32[]{:S(2)}) collective-permute-start(bf16[256,512]{0,1:T(8,128)(2,1)S(1)} %bitcast.81), channel_id=1, source_target_pairs={{0,24},{8,32},{16,40},{24,48},{32,56},{40,64},{48,72},{56,80},{64,... | collective-permute-start | bytes 786440 | tf_op jit(solution)/shard_map/ppermute | solution.py:15
  13.9 3.2 %collective-permute-start.2 = (bf16[256,512]{0,1:T(8,128)(2,1)S(1)}, bf16[256,512]{0,1:T(8,128)(2,1)}, u32[]{:S(2)}, u32[]{:S(2)}) collective-permute-start(bf16[256,512]{0,1:T(8,128)(2,1)S(1)} %bitcast.82), channel_id=1, source_target_pairs={{0,16},{8,24},{16,32},{24,40},{32,48},{40,56},{48,64},{56,72},{64,... | collective-permute-start | bytes 786440 | tf_op jit(solution)/shard_map/ppermute | solution.py:15
  17.1 1.9 collective-permute-start.3
  19.2 4.7 %collective-permute-start.4 = (bf16[256,512]{0,1:T(8,128)(2,1)S(1)}, bf16[256,512]{0,1:T(8,128)(2,1)}, u32[]{:S(2)}, u32[]{:S(2)}) collective-permute-start(bf16[256,512]{0,1:T(8,128)(2,1)S(1)} %bitcast.85), channel_id=1, source_target_pairs={{0,32},{8,40},{16,48},{24,56},{32,64},{40,72},{48,80},{56,88},{64,... | collective-permute-start | bytes 786440 | tf_op jit(solution)/shard_map/ppermute | solution.py:15
  30.3 3.4 %collective-permute-start.5 = (bf16[256,512]{0,1:T(8,128)(2,1)S(1)}, bf16[256,512]{0,1:T(8,128)(2,1)S(1)}, u32[]{:S(2)}, u32[]{:S(2)}) collective-permute-start(bf16[256,512]{0,1:T(8,128)(2,1)S(1)} %bitcast.87), channel_id=1, source_target_pairs={{0,24},{8,32},{16,40},{24,48},{32,56},{40,64},{48,72},{56,80},{64,... | collective-permute-start | bytes 786440 | tf_op jit(solution)/shard_map/ppermute | solution.py:15
  34.6 3.9 %collective-permute-start.6 = (bf16[256,512]{0,1:T(8,128)(2,1)S(1)}, bf16[256,512]{0,1:T(8,128)(2,1)}, u32[]{:S(2)}, u32[]{:S(2)}) collective-permute-start(bf16[256,512]{0,1:T(8,128)(2,1)S(1)} %bitcast.88), channel_id=1, source_target_pairs={{0,16},{8,24},{16,32},{24,40},{32,48},{40,56},{48,64},{56,72},{64,... | collective-permute-start | bytes 786440 | tf_op jit(solution)/shard_map/ppermute | solution.py:15
  39.5 2.2 collective-permute-start.7
  47.6 1.8 copy.112
  52.0 3.0 %fusion.39 = (f32[2,2,256]{2,1,0:T(2,128)S(1)}, f32[2,2,256,1280]{2,3,1,0:T(8,128)S(1)}) fusion(bf16[1280,2,256,1]{0,2,3,1:T(8,128)(2,1)} %bitcast.94, bf16[256,2,2,256]{3,0,2,1:T(8,128)(2,1)} %bitcast.91, pred[256,1280]{0,1:T(8,128)(4,1)} %fusion.20), kind=kOutput, calls=%fused_computation.89 | convolution fusion | flops 675019776 | bytes 7409664 | tf_op jit(solution)/shard_map/tkgd,skd->kgts/dot_general | solution.py:87
  55.7 1.7 copy-done
  57.8 3.2 %fusion.15 = f32[2,1280,256,2]{2,1,3,0:T(8,128)} fusion(bf16[256,2,2,256]{0,3,2,1:T(8,128)(2,1)S(1)} %bitcast.76, bf16[1280,2,256]{2,0,1:T(8,128)(2,1)S(1)} %constant_dynamic-update-slice_fusion.5), kind=kOutput, calls=%fused_computation.20 | convolution fusion | flops 671088640 | bytes 7077888 | tf_op jit(solution)/shard_map/tkgd,skd->kgts/dot_general | solution.py:95
  61.0 10.9 %fusion.6 = f32[2,256,2,256]{3,1,2,0:T(8,128)} fusion(bf16[1280,2,256,1]{0,2,3,1:T(8,128)(2,1)} %bitcast.95, f32[2,1280,256,2]{2,1,3,0:T(8,128)} %fusion.15, f32[2,2,256,1280]{2,3,1,0:T(8,128)} %copy-done, f32[2,2,256]{2,1,0:T(2,128)S(1)} %log_add_fusion), kind=kOutput, calls=%fused_computation.13 | convolution fusion | flops 680265984 | bytes 12849152 | tf_op jit(solution)/shard_map/kgts,skd->tkgd/dot_general | solution.py:98
  71.8 11.7 %fusion.40 = (bf16[1280,2,256]{0,2,1:T(8,128)(2,1)}, f32[1280,2,256]{0,2,1:T(8,128)}) fusion(bf16[256,2,2,256]{3,0,2,1:T(8,128)(2,1)S(1)} %bitcast.92, f32[2,1280,256,2]{2,1,3,0:T(8,128)} %fusion.15, f32[2,2,256,1280]{2,3,1,0:T(8,128)} %copy-done, f32[2,2,256]{2,1,0:T(2,128)S(1)} %log_add_fusion), kind=kOutput, calls=%fused_computation.90 | convolution fusion | flops 680921344 | bytes 14946304 | tf_op jit(solution)/shard_map/kgts,tkgd->skd/dot_general | solution.py:101
  83.6 5.4 %fusion.41 = (bf16[1280,2,256]{0,2,1:T(8,128)(2,1)}, f32[1280,2,256]{0,2,1:T(8,128)}) fusion(bf16[256,2,2,256]{0,3,2,1:T(8,128)(2,1)S(1)} %bitcast.77, f32[2,2,256,1280]{2,3,1,0:T(8,128)} %copy-done, f32[2,2,256]{2,1,0:T(2,128)S(1)} %log_add_fusion), kind=kOutput, calls=%fused_computation.91 | convolution fusion | flops 674365440 | bytes 9703424 | tf_op jit(solution)/shard_map/kgts,tkgd->skd/dot_general | solution.py:102
  90.3 1.4 multiply_add_fusion.1
  93.9 2.2 fusion.37
  96.0 1.3 collective-permute-start.11
  97.3 1.3 collective-permute-start.10
  98.6 1.3 collective-permute-start.9
  99.9 3.1 %collective-permute-start.8 = (bf16[256,2,256]{0,2,1:T(8,128)(2,1)}, bf16[256,2,256]{0,2,1:T(8,128)(2,1)}, u32[]{:S(2)}, u32[]{:S(2)}) collective-permute-start(bf16[256,2,256]{0,2,1:T(8,128)(2,1)} %get-tuple-element.40), channel_id=1, source_target_pairs={{8,0},{16,8},{24,16},{32,24},{40,32},{48,40},{56,48},{64,56},{72,6... | collective-permute-start | bytes 786440 | tf_op jit(solution)/shard_map/ppermute | solution.py:15
  103.0 1.6 fusion.21
  105.7 2.1 fusion.36
  109.1 1.3 collective-permute-start.14
  110.6 1.3 collective-permute-start.13
  111.9 10.3 %collective-permute-done.9 = bf16[256,2,256]{0,2,1:T(8,128)(2,1)} collective-permute-done((bf16[256,2,256]{0,2,1:T(8,128)(2,1)}, bf16[256,2,256]{0,2,1:T(8,128)(2,1)}, u32[]{:S(2)}, u32[]{:S(2)}) %collective-permute-start.9) | collective-permute-done | bytes 262176 | tf_op jit(solution)/shard_map/ppermute | solution.py:15
  122.1 1.9 collective-permute-start.12
  124.0 6.9 %collective-permute-done.8 = bf16[256,2,256]{0,2,1:T(8,128)(2,1)} collective-permute-done((bf16[256,2,256]{0,2,1:T(8,128)(2,1)}, bf16[256,2,256]{0,2,1:T(8,128)(2,1)}, u32[]{:S(2)}, u32[]{:S(2)}) %collective-permute-start.8) | collective-permute-done | bytes 262176 | tf_op jit(solution)/shard_map/ppermute | solution.py:15
  131.0 1.5 fusion.29
  133.7 6.3 %collective-permute-done.13 = bf16[256,2,256]{0,2,1:T(8,128)(2,1)S(1)} collective-permute-done((bf16[256,2,256]{0,2,1:T(8,128)(2,1)S(1)}, bf16[256,2,256]{0,2,1:T(8,128)(2,1)S(1)}, u32[]{:S(2)}, u32[]{:S(2)}) %collective-permute-start.13) | collective-permute-done | bytes 262176 | tf_op jit(solution)/shard_map/ppermute | solution.py:15
  140.0 1.9 collective-permute-done.12
  144.0 114.1 %all-reduce.4 = (f32[256]{0:T(256)}, f32[256]{0:T(256)}) all-reduce(f32[256]{0:T(256)S(1)} %copy-done.15, f32[256]{0:T(256)S(1)} %get-tuple-element.32), channel_id=1, replica_groups=mesh['seq'=64,'dp'=8] {'seq','dp'}, use_global_device_ids=true, to_apply=%region_8.9 | all-reduce | flops 512 | bytes 4096 | tf_op jit(solution)/shard_map/psum | solution.py:115
  (100 shorter events, 29.8 us)
Async XLA Ops:
  0.6 18.4 %copy-start.9 = (bf16[1,256,512]{2,1,0:T(8,128)(2,1)S(1)}, bf16[1,256,512]{2,1,0:T(8,128)(2,1)}, u32[]{:S(2)}) copy-start(bf16[1,256,512]{2,1,0:T(8,128)(2,1)} %param.8) | copy-start | bytes 786436
  0.7 23.5 %copy-start.7 = (bf16[1,256,1024]{2,1,0:T(8,128)(2,1)S(1)}, bf16[1,256,1024]{2,1,0:T(8,128)(2,1)}, u32[]{:S(2)}) copy-start(bf16[1,256,1024]{2,1,0:T(8,128)(2,1)} %param.6) | copy-start | bytes 1572868
  3.2 22.0 %copy-start.12 = (f32[256]{0:T(256)S(1)}, f32[256]{0:T(256)}, u32[]{:S(2)}) copy-start(f32[256]{0:T(256)} %param.10) | copy-start | bytes 3076
  3.4 26.9 %collective-permute-start = (bf16[256,512]{0,1:T(8,128)(2,1)S(1)}, bf16[256,512]{0,1:T(8,128)(2,1)}, u32[]{:S(2)}, u32[]{:S(2)}) collective-permute-start(bf16[256,512]{0,1:T(8,128)(2,1)S(1)} %bitcast.80), channel_id=1, source_target_pairs={{0,32},{8,40},{16,48},{24,56},{32,64},{40,72},{48,80},{56,88},{64,... | collective-permute-start | bytes 786440 | tf_op jit(solution)/shard_map/ppermute | solution.py:15
  9.7 24.9 %collective-permute-start.1 = (bf16[256,512]{0,1:T(8,128)(2,1)S(1)}, bf16[256,512]{0,1:T(8,128)(2,1)}, u32[]{:S(2)}, u32[]{:S(2)}) collective-permute-start(bf16[256,512]{0,1:T(8,128)(2,1)S(1)} %bitcast.81), channel_id=1, source_target_pairs={{0,24},{8,32},{16,40},{24,48},{32,56},{40,64},{48,72},{56,80},{64,... | collective-permute-start | bytes 786440 | tf_op jit(solution)/shard_map/ppermute | solution.py:15
  13.9 25.6 %collective-permute-start.2 = (bf16[256,512]{0,1:T(8,128)(2,1)S(1)}, bf16[256,512]{0,1:T(8,128)(2,1)}, u32[]{:S(2)}, u32[]{:S(2)}) collective-permute-start(bf16[256,512]{0,1:T(8,128)(2,1)S(1)} %bitcast.82), channel_id=1, source_target_pairs={{0,16},{8,24},{16,32},{24,40},{32,48},{40,56},{48,64},{56,72},{64,... | collective-permute-start | bytes 786440 | tf_op jit(solution)/shard_map/ppermute | solution.py:15
  17.1 25.6 %collective-permute-start.3 = (bf16[256,512]{0,1:T(8,128)(2,1)S(1)}, bf16[256,512]{0,1:T(8,128)(2,1)}, u32[]{:S(2)}, u32[]{:S(2)}) collective-permute-start(bf16[256,512]{0,1:T(8,128)(2,1)S(1)} %bitcast.83), channel_id=1, source_target_pairs={{0,8},{8,16},{16,24},{24,32},{32,40},{40,48},{48,56},{56,64},{64,7... | collective-permute-start | bytes 786440 | tf_op jit(solution)/shard_map/ppermute | solution.py:15
  19.2 24.5 %collective-permute-start.4 = (bf16[256,512]{0,1:T(8,128)(2,1)S(1)}, bf16[256,512]{0,1:T(8,128)(2,1)}, u32[]{:S(2)}, u32[]{:S(2)}) collective-permute-start(bf16[256,512]{0,1:T(8,128)(2,1)S(1)} %bitcast.85), channel_id=1, source_target_pairs={{0,32},{8,40},{16,48},{24,56},{32,64},{40,72},{48,80},{56,88},{64,... | collective-permute-start | bytes 786440 | tf_op jit(solution)/shard_map/ppermute | solution.py:15
  24.0 2.7 %copy-start.2 = (f32[256,128]{1,0:T(8,128)}, f32[256,128]{1,0:T(8,128)S(1)}, u32[]{:S(2)}) copy-start(f32[256,128]{1,0:T(8,128)S(1)} %copy.105) | copy-start | bytes 393220
  24.1 2.6 %copy-start.3 = (f32[256,128]{1,0:T(8,128)}, f32[256,128]{1,0:T(8,128)S(1)}, u32[]{:S(2)}) copy-start(f32[256,128]{1,0:T(8,128)S(1)} %copy.104) | copy-start | bytes 393220
  30.3 15.6 %collective-permute-start.5 = (bf16[256,512]{0,1:T(8,128)(2,1)S(1)}, bf16[256,512]{0,1:T(8,128)(2,1)S(1)}, u32[]{:S(2)}, u32[]{:S(2)}) collective-permute-start(bf16[256,512]{0,1:T(8,128)(2,1)S(1)} %bitcast.87), channel_id=1, source_target_pairs={{0,24},{8,32},{16,40},{24,48},{32,56},{40,64},{48,72},{56,80},{64,... | collective-permute-start | bytes 786440 | tf_op jit(solution)/shard_map/ppermute | solution.py:15
  34.6 13.0 %collective-permute-start.6 = (bf16[256,512]{0,1:T(8,128)(2,1)S(1)}, bf16[256,512]{0,1:T(8,128)(2,1)}, u32[]{:S(2)}, u32[]{:S(2)}) collective-permute-start(bf16[256,512]{0,1:T(8,128)(2,1)S(1)} %bitcast.88), channel_id=1, source_target_pairs={{0,16},{8,24},{16,32},{24,40},{32,48},{40,56},{48,64},{56,72},{64,... | collective-permute-start | bytes 786440 | tf_op jit(solution)/shard_map/ppermute | solution.py:15
  39.5 11.4 %collective-permute-start.7 = (bf16[256,512]{0,1:T(8,128)(2,1)S(1)}, bf16[256,512]{0,1:T(8,128)(2,1)}, u32[]{:S(2)}, u32[]{:S(2)}) collective-permute-start(bf16[256,512]{0,1:T(8,128)(2,1)S(1)} %bitcast.89), channel_id=1, source_target_pairs={{0,8},{8,16},{16,24},{24,32},{32,40},{40,48},{48,56},{56,64},{64,7... | collective-permute-start | bytes 786440 | tf_op jit(solution)/shard_map/ppermute | solution.py:15
  43.6 1.1 copy-start.11
  45.8 0.7 copy-start.10
  55.0 2.4 copy-start
  55.0 2.4 copy-start.1
  55.0 2.5 copy-start.6
  55.0 2.8 %copy-start.5 = (bf16[256,2,256]{2,0,1:T(8,128)(2,1)S(1)}, bf16[256,2,256]{2,0,1:T(8,128)(2,1)}, u32[]{:S(2)}) copy-start(bf16[256,2,256]{2,0,1:T(8,128)(2,1)} %copy.114) | copy-start | bytes 786436
  61.0 10.9 %copy-start.8 = (bf16[256,4,256]{2,0,1:T(8,128)(2,1)S(1)}, bf16[256,4,256]{2,0,1:T(8,128)(2,1)}, u32[]{:S(2)}) copy-start(bf16[256,4,256]{2,0,1:T(8,128)(2,1)} %copy.106) | copy-start | bytes 1572868
  83.5 5.4 %copy-start.4 = (f32[2,256,2,256]{3,1,2,0:T(8,128)S(1)}, f32[2,256,2,256]{3,1,2,0:T(8,128)}, u32[]{:S(2)}) copy-start(f32[2,256,2,256]{3,1,2,0:T(8,128)} %fusion.6) | copy-start | bytes 3145732
  89.0 2.7 %copy-start.13 = (f32[256]{0:T(256)S(1)}, f32[256]{0:T(256)}, u32[]{:S(2)}) copy-start(f32[256]{0:T(256)} %param.10) | copy-start | bytes 3076
  96.0 13.1 %collective-permute-start.11 = (bf16[256,2,256]{0,2,1:T(8,128)(2,1)}, bf16[256,2,256]{0,2,1:T(8,128)(2,1)}, u32[]{:S(2)}, u32[]{:S(2)}) collective-permute-start(bf16[256,2,256]{0,2,1:T(8,128)(2,1)} %get-tuple-element.41), channel_id=1, source_target_pairs={{32,0},{40,8},{48,16},{56,24},{64,32},{72,40},{80,48},{88,56},{96,... | collective-permute-start | bytes 786440 | tf_op jit(solution)/shard_map/ppermute | solution.py:15
  97.3 13.3 %collective-permute-start.10 = (bf16[256,2,256]{0,2,1:T(8,128)(2,1)}, bf16[256,2,256]{0,2,1:T(8,128)(2,1)}, u32[]{:S(2)}, u32[]{:S(2)}) collective-permute-start(bf16[256,2,256]{0,2,1:T(8,128)(2,1)} %get-tuple-element.42), channel_id=1, source_target_pairs={{24,0},{32,8},{40,16},{48,24},{56,32},{64,40},{72,48},{80,56},{88,... | collective-permute-start | bytes 786440 | tf_op jit(solution)/shard_map/ppermute | solution.py:15
  98.6 23.5 %collective-permute-start.9 = (bf16[256,2,256]{0,2,1:T(8,128)(2,1)}, bf16[256,2,256]{0,2,1:T(8,128)(2,1)}, u32[]{:S(2)}, u32[]{:S(2)}) collective-permute-start(bf16[256,2,256]{0,2,1:T(8,128)(2,1)} %get-tuple-element.43), channel_id=1, source_target_pairs={{16,0},{24,8},{32,16},{40,24},{48,32},{56,40},{64,48},{72,56},{80,... | collective-permute-start | bytes 786440 | tf_op jit(solution)/shard_map/ppermute | solution.py:15
  99.9 31.0 %collective-permute-start.8 = (bf16[256,2,256]{0,2,1:T(8,128)(2,1)}, bf16[256,2,256]{0,2,1:T(8,128)(2,1)}, u32[]{:S(2)}, u32[]{:S(2)}) collective-permute-start(bf16[256,2,256]{0,2,1:T(8,128)(2,1)} %get-tuple-element.40), channel_id=1, source_target_pairs={{8,0},{16,8},{24,16},{32,24},{40,32},{48,40},{56,48},{64,56},{72,6... | collective-permute-start | bytes 786440 | tf_op jit(solution)/shard_map/ppermute | solution.py:15
  105.7 26.8 %copy-start.14 = (f32[256]{0:T(256)S(1)}, f32[256]{0:T(256)}, u32[]{:S(2)}) copy-start(f32[256]{0:T(256)} %param.11) | copy-start | bytes 3076
  107.8 25.9 %collective-permute-start.15 = (bf16[256,2,256]{0,2,1:T(8,128)(2,1)}, bf16[256,2,256]{0,2,1:T(8,128)(2,1)S(1)}, u32[]{:S(2)}, u32[]{:S(2)}) collective-permute-start(bf16[256,2,256]{0,2,1:T(8,128)(2,1)} %get-tuple-element.37), channel_id=1, source_target_pairs={{32,0},{40,8},{48,16},{56,24},{64,32},{72,40},{80,48},{88,56},{96,... | collective-permute-start | bytes 786440 | tf_op jit(solution)/shard_map/ppermute | solution.py:15
  109.1 24.6 %collective-permute-start.14 = (bf16[256,2,256]{0,2,1:T(8,128)(2,1)}, bf16[256,2,256]{0,2,1:T(8,128)(2,1)S(1)}, u32[]{:S(2)}, u32[]{:S(2)}) collective-permute-start(bf16[256,2,256]{0,2,1:T(8,128)(2,1)} %get-tuple-element.38), channel_id=1, source_target_pairs={{24,0},{32,8},{40,16},{48,24},{56,32},{64,40},{72,48},{80,56},{88,... | collective-permute-start | bytes 786440 | tf_op jit(solution)/shard_map/ppermute | solution.py:15
  110.6 29.5 %collective-permute-start.13 = (bf16[256,2,256]{0,2,1:T(8,128)(2,1)S(1)}, bf16[256,2,256]{0,2,1:T(8,128)(2,1)S(1)}, u32[]{:S(2)}, u32[]{:S(2)}) collective-permute-start(bf16[256,2,256]{0,2,1:T(8,128)(2,1)S(1)} %get-tuple-element.39), channel_id=1, source_target_pairs={{16,0},{24,8},{32,16},{40,24},{48,32},{56,40},{64,48},{72,56},{80,... | collective-permute-start | bytes 786440 | tf_op jit(solution)/shard_map/ppermute | solution.py:15
  122.1 19.9 %collective-permute-start.12 = (bf16[256,2,256]{0,2,1:T(8,128)(2,1)S(1)}, bf16[256,2,256]{0,2,1:T(8,128)(2,1)S(1)}, u32[]{:S(2)}, u32[]{:S(2)}) collective-permute-start(bf16[256,2,256]{0,2,1:T(8,128)(2,1)S(1)} %get-tuple-element.36), channel_id=1, source_target_pairs={{8,0},{16,8},{24,16},{32,24},{40,32},{48,40},{56,48},{64,56},{72,6... | collective-permute-start | bytes 786440 | tf_op jit(solution)/shard_map/ppermute | solution.py:15
  132.5 11.5 %copy-start.15 = (f32[256]{0:T(256)S(1)}, f32[256]{0:T(256)}, u32[]{:S(2)}) copy-start(f32[256]{0:T(256)} %get-tuple-element.30) | copy-start | bytes 3076
where the time goes:
time: 259 us; the launch traced here: 258 us
  blocking collectives  114 us (44%)
  starting transfers between devices  42.5 us (16%)
  matrix products  34.2 us (13%)
  local copies, waits for them, and re-layouts  28.6 us (11%)
  waiting for transfers between devices  25.6 us (10%)
  other arithmetic  11.9 us (5%)
    psum x1, blocking collectives, local(): lax.psum((gain_q_local, gain_k_local), ('seq', 'dp'))  114 us
    ppermute x16, starting transfers between devices, from_behind(): return lax.ppermute(array, axis, pairs)  42.5 us
    ppermute x16, waiting for transfers between devices, from_behind(): return lax.ppermute(array, axis, pairs)  25.6 us
    dot_general x1, matrix products, local(): jnp.einsum('kgts,tkgd->skd', dscores, q_heads, preferred_element_type=jnp...  11.7 us
    unnamed x45, local copies, waits for them, and re-layouts  11.5 us
    dot_general x1, matrix products, local(): jnp.einsum('kgts,skd->tkgd', dscores, k_heads, preferred_element_type=jnp...  10.9 us
    concatenate x6, local copies, waits for them, and re-layouts, local(): value_rows = jnp.concatenate(halo_v + [v_local], axis=0)  5.89 us
    dot_general x1, matrix products, local(): jnp.einsum('kgts,tkgd->skd', weights_b, do_heads, preferred_element_type=...  5.41 us
  transfers between devices with their start and end apart: 16, of which 5 were waited for; matrix products, arithmetic and copies ran while one was open for 9% of the time, Pallas kernels for 0%

commit v1 on v0

--- a/solution.py
+++ b/solution.py
@@ -112,7 +112,7 @@
     dk_rot = dk_own.reshape(rows_here, pair_heads * head_size)
     grad_q_local, gain_q_local = q_back(dq_rot)
     grad_k_local, gain_k_local = k_back(dk_rot)
-    gain_q_all, gain_k_all = lax.psum((gain_q_local, gain_k_local), ("seq", "dp"))
+    gain_q_all, gain_k_all = lax.psum(lax.psum((gain_q_local, gain_k_local), "seq"), "dp")
     grad_v_local = dv_own.reshape(rows_here, pair_heads * head_size).astype(jnp.bfloat16)
     return (
         grad_q_local.astype(jnp.bfloat16)[None],

time: 259 us -> 401 us (1.55); the launches traced: 258 us -> 395 us
  blocking collectives: 114 us -> 251 us
    psum x1 -> x2, blocking collectives: 114 us -> 251 us  [the longest x1 213 us: local(): lax.psum((gain_q_local, gain_k_local), 'seq')]
  transfers between devices with their start and end apart: 16 -> 16, of which waited for: 5 -> 5; matrix products, arithmetic and copies ran while one was open for 9% -> 6% of each run, Pallas kernels for 0% -> 0%
where the time goes in v1:
time: 401 us; the launch traced here: 395 us
  blocking collectives  251 us (63%)
  starting transfers between devices  42.5 us (11%)
  matrix products  34.2 us (9%)
  local copies, waits for them, and re-layouts  27.8 us (7%)
  waiting for transfers between devices  26.4 us (7%)
  other arithmetic  11.9 us (3%)
    psum x1, blocking collectives, local(): lax.psum((gain_q_local, gain_k_local), 'seq')  213 us
    ppermute x16, starting transfers between devices, from_behind(): return lax.ppermute(array, axis, pairs)  42.5 us
    psum x1, blocking collectives, local(): lax.psum(lax.psum((gain_q_local, gain_k_local), 'seq'), 'dp')  38.7 us
    ppermute x16, waiting for transfers between devices, from_behind(): return lax.ppermute(array, axis, pairs)  26.4 us
    dot_general x1, matrix products, local(): jnp.einsum('kgts,tkgd->skd', dscores, q_heads, preferred_element_type=jnp...  11.7 us
    unnamed x45, local copies, waits for them, and re-layouts  11.5 us
    dot_general x1, matrix products, local(): jnp.einsum('kgts,skd->tkgd', dscores, k_heads, preferred_element_type=jnp...  10.9 us
  transfers between devices with their start and end apart: 16, of which 5 were waited for; matrix products, arithmetic and copies ran while one was open for 6% of the time, Pallas kernels for 0%

profile of v1, /device:TPU:1, one launch (start us, length us, event | category | flops | bytes accessed | tf_op | source)
XLA Modules:
  0.0 395.4 jit_solution(4796626749913352979)
XLA Ops:
  3.4 6.4 %collective-permute-start = (bf16[256,512]{0,1:T(8,128)(2,1)S(1)}, bf16[256,512]{0,1:T(8,128)(2,1)}, u32[]{:S(2)}, u32[]{:S(2)}) collective-permute-start(bf16[256,512]{0,1:T(8,128)(2,1)S(1)} %bitcast.80), channel_id=1, source_target_pairs={{0,32},{8,40},{16,48},{24,56},{32,64},{40,72},{48,80},{56,88},{64,... | collective-permute-start | bytes 786440 | tf_op jit(solution)/shard_map/ppermute | solution.py:15
  9.7 4.2 %collective-permute-start.1 = (bf16[256,512]{0,1:T(8,128)(2,1)S(1)}, bf16[256,512]{0,1:T(8,128)(2,1)}, u32[]{:S(2)}, u32[]{:S(2)}) collective-permute-start(bf16[256,512]{0,1:T(8,128)(2,1)S(1)} %bitcast.81), channel_id=1, source_target_pairs={{0,24},{8,32},{16,40},{24,48},{32,56},{40,64},{48,72},{56,80},{64,... | collective-permute-start | bytes 786440 | tf_op jit(solution)/shard_map/ppermute | solution.py:15
  13.9 3.2 collective-permute-start.2
  17.1 1.9 collective-permute-start.3
  19.2 4.7 %collective-permute-start.4 = (bf16[256,512]{0,1:T(8,128)(2,1)S(1)}, bf16[256,512]{0,1:T(8,128)(2,1)}, u32[]{:S(2)}, u32[]{:S(2)}) collective-permute-start(bf16[256,512]{0,1:T(8,128)(2,1)S(1)} %bitcast.85), channel_id=1, source_target_pairs={{0,32},{8,40},{16,48},{24,56},{32,64},{40,72},{48,80},{56,88},{64,... | collective-permute-start | bytes 786440 | tf_op jit(solution)/shard_map/ppermute | solution.py:15
  30.2 3.4 collective-permute-start.5
  34.6 3.9 collective-permute-start.6
  39.5 2.2 collective-permute-start.7
  47.6 1.8 copy.112
  52.0 3.0 fusion.39
  55.7 1.7 copy-done
  57.8 3.2 fusion.15
  61.0 10.9 %fusion.6 = f32[2,256,2,256]{3,1,2,0:T(8,128)} fusion(bf16[1280,2,256,1]{0,2,3,1:T(8,128)(2,1)} %bitcast.95, f32[2,1280,256,2]{2,1,3,0:T(8,128)} %fusion.15, f32[2,2,256,1280]{2,3,1,0:T(8,128)} %copy-done, f32[2,2,256]{2,1,0:T(2,128)S(1)} %log_add_fusion), kind=kOutput, calls=%fused_computation.13 | convolution fusion | flops 680265984 | bytes 12849152 | tf_op jit(solution)/shard_map/kgts,skd->tkgd/dot_general | solution.py:98
  71.8 11.7 %fusion.40 = (bf16[1280,2,256]{0,2,1:T(8,128)(2,1)}, f32[1280,2,256]{0,2,1:T(8,128)}) fusion(bf16[256,2,2,256]{3,0,2,1:T(8,128)(2,1)S(1)} %bitcast.92, f32[2,1280,256,2]{2,1,3,0:T(8,128)} %fusion.15, f32[2,2,256,1280]{2,3,1,0:T(8,128)} %copy-done, f32[2,2,256]{2,1,0:T(2,128)S(1)} %log_add_fusion), kind=kOutput, calls=%fused_computation.90 | convolution fusion | flops 680921344 | bytes 14946304 | tf_op jit(solution)/shard_map/kgts,tkgd->skd/dot_general | solution.py:101
  83.6 5.4 %fusion.41 = (bf16[1280,2,256]{0,2,1:T(8,128)(2,1)}, f32[1280,2,256]{0,2,1:T(8,128)}) fusion(bf16[256,2,2,256]{0,3,2,1:T(8,128)(2,1)S(1)} %bitcast.77, f32[2,2,256,1280]{2,3,1,0:T(8,128)} %copy-done, f32[2,2,256]{2,1,0:T(2,128)S(1)} %log_add_fusion), kind=kOutput, calls=%fused_computation.91 | convolution fusion | flops 674365440 | bytes 9703424 | tf_op jit(solution)/shard_map/kgts,tkgd->skd/dot_general | solution.py:102
  90.3 1.4 multiply_add_fusion.1
  93.9 2.2 fusion.37
  97.3 1.3 collective-permute-start.10
  98.6 1.3 collective-permute-start.9
  99.9 3.1 collective-permute-start.8
  103.0 1.6 fusion.21
  107.0 1.3 collective-permute-start.15
  108.3 1.3 collective-permute-start.14
  110.6 1.3 collective-permute-start.13
  111.9 11.5 %collective-permute-done.9 = bf16[256,2,256]{0,2,1:T(8,128)(2,1)} collective-permute-done((bf16[256,2,256]{0,2,1:T(8,128)(2,1)}, bf16[256,2,256]{0,2,1:T(8,128)(2,1)}, u32[]{:S(2)}, u32[]{:S(2)}) %collective-permute-start.9) | collective-permute-done | bytes 262176 | tf_op jit(solution)/shard_map/ppermute | solution.py:15
  123.3 1.9 collective-permute-start.12
  125.2 6.9 %collective-permute-done.8 = bf16[256,2,256]{0,2,1:T(8,128)(2,1)} collective-permute-done((bf16[256,2,256]{0,2,1:T(8,128)(2,1)}, bf16[256,2,256]{0,2,1:T(8,128)(2,1)}, u32[]{:S(2)}, u32[]{:S(2)}) %collective-permute-start.8) | collective-permute-done | bytes 262176 | tf_op jit(solution)/shard_map/ppermute | solution.py:15
  132.2 1.5 fusion.29
  135.0 5.1 %collective-permute-done.13 = bf16[256,2,256]{0,2,1:T(8,128)(2,1)S(1)} collective-permute-done((bf16[256,2,256]{0,2,1:T(8,128)(2,1)S(1)}, bf16[256,2,256]{0,2,1:T(8,128)(2,1)S(1)}, u32[]{:S(2)}, u32[]{:S(2)}) %collective-permute-start.13) | collective-permute-done | bytes 262176 | tf_op jit(solution)/shard_map/ppermute | solution.py:15
  140.0 1.9 collective-permute-done.12
  144.0 212.7 %all-reduce.4 = (f32[256]{0:T(256)S(1)}, f32[256]{0:T(256)S(1)}) all-reduce(f32[256]{0:T(256)S(1)} %copy-done.15, f32[256]{0:T(256)S(1)} %get-tuple-element.32), channel_id=1, replica_groups=mesh['seq'=64,'dp'=8] {'seq'}, use_global_device_ids=true, to_apply=%region_8.9 | all-reduce | flops 512 | bytes 4096 | tf_op jit(solution)/shard_map/psum | solution.py:115
  356.7 38.7 %all-reduce.5 = (f32[256]{0:T(256)}, f32[256]{0:T(256)}) all-reduce(f32[256]{0:T(256)S(1)} %get-tuple-element.34, f32[256]{0:T(256)S(1)} %get-tuple-element.35), channel_id=1, replica_groups=mesh['seq'=64,'dp'=8] {'dp'}, use_global_device_ids=true, to_apply=%region_9.10 | all-reduce | flops 512 | bytes 4096 | tf_op jit(solution)/shard_map/psum | solution.py:115
  (101 shorter events, 31.8 us)
Async XLA Ops:
  0.6 18.4 %copy-start.9 = (bf16[1,256,512]{2,1,0:T(8,128)(2,1)S(1)}, bf16[1,256,512]{2,1,0:T(8,128)(2,1)}, u32[]{:S(2)}) copy-start(bf16[1,256,512]{2,1,0:T(8,128)(2,1)} %param.8) | copy-start | bytes 786436
  0.7 23.5 %copy-start.7 = (bf16[1,256,1024]{2,1,0:T(8,128)(2,1)S(1)}, bf16[1,256,1024]{2,1,0:T(8,128)(2,1)}, u32[]{:S(2)}) copy-start(bf16[1,256,1024]{2,1,0:T(8,128)(2,1)} %param.6) | copy-start | bytes 1572868
  3.2 22.0 %copy-start.12 = (f32[256]{0:T(256)S(1)}, f32[256]{0:T(256)}, u32[]{:S(2)}) copy-start(f32[256]{0:T(256)} %param.10) | copy-start | bytes 3076
  3.4 26.9 %collective-permute-start = (bf16[256,512]{0,1:T(8,128)(2,1)S(1)}, bf16[256,512]{0,1:T(8,128)(2,1)}, u32[]{:S(2)}, u32[]{:S(2)}) collective-permute-start(bf16[256,512]{0,1:T(8,128)(2,1)S(1)} %bitcast.80), channel_id=1, source_target_pairs={{0,32},{8,40},{16,48},{24,56},{32,64},{40,72},{48,80},{56,88},{64,... | collective-permute-start | bytes 786440 | tf_op jit(solution)/shard_map/ppermute | solution.py:15
  9.7 24.9 %collective-permute-start.1 = (bf16[256,512]{0,1:T(8,128)(2,1)S(1)}, bf16[256,512]{0,1:T(8,128)(2,1)}, u32[]{:S(2)}, u32[]{:S(2)}) collective-permute-start(bf16[256,512]{0,1:T(8,128)(2,1)S(1)} %bitcast.81), channel_id=1, source_target_pairs={{0,24},{8,32},{16,40},{24,48},{32,56},{40,64},{48,72},{56,80},{64,... | collective-permute-start | bytes 786440 | tf_op jit(solution)/shard_map/ppermute | solution.py:15
  13.9 25.6 %collective-permute-start.2 = (bf16[256,512]{0,1:T(8,128)(2,1)S(1)}, bf16[256,512]{0,1:T(8,128)(2,1)}, u32[]{:S(2)}, u32[]{:S(2)}) collective-permute-start(bf16[256,512]{0,1:T(8,128)(2,1)S(1)} %bitcast.82), channel_id=1, source_target_pairs={{0,16},{8,24},{16,32},{24,40},{32,48},{40,56},{48,64},{56,72},{64,... | collective-permute-start | bytes 786440 | tf_op jit(solution)/shard_map/ppermute | solution.py:15
  17.1 25.5 %collective-permute-start.3 = (bf16[256,512]{0,1:T(8,128)(2,1)S(1)}, bf16[256,512]{0,1:T(8,128)(2,1)}, u32[]{:S(2)}, u32[]{:S(2)}) collective-permute-start(bf16[256,512]{0,1:T(8,128)(2,1)S(1)} %bitcast.83), channel_id=1, source_target_pairs={{0,8},{8,16},{16,24},{24,32},{32,40},{40,48},{48,56},{56,64},{64,7... | collective-permute-start | bytes 786440 | tf_op jit(solution)/shard_map/ppermute | solution.py:15
  19.2 24.5 %collective-permute-start.4 = (bf16[256,512]{0,1:T(8,128)(2,1)S(1)}, bf16[256,512]{0,1:T(8,128)(2,1)}, u32[]{:S(2)}, u32[]{:S(2)}) collective-permute-start(bf16[256,512]{0,1:T(8,128)(2,1)S(1)} %bitcast.85), channel_id=1, source_target_pairs={{0,32},{8,40},{16,48},{24,56},{32,64},{40,72},{48,80},{56,88},{64,... | collective-permute-start | bytes 786440 | tf_op jit(solution)/shard_map/ppermute | solution.py:15
  24.0 2.7 copy-start.2
  24.1 2.6 copy-start.3
  30.2 15.6 %collective-permute-start.5 = (bf16[256,512]{0,1:T(8,128)(2,1)S(1)}, bf16[256,512]{0,1:T(8,128)(2,1)S(1)}, u32[]{:S(2)}, u32[]{:S(2)}) collective-permute-start(bf16[256,512]{0,1:T(8,128)(2,1)S(1)} %bitcast.87), channel_id=1, source_target_pairs={{0,24},{8,32},{16,40},{24,48},{32,56},{40,64},{48,72},{56,80},{64,... | collective-permute-start | bytes 786440 | tf_op jit(solution)/shard_map/ppermute | solution.py:15
  34.6 13.0 %collective-permute-start.6 = (bf16[256,512]{0,1:T(8,128)(2,1)S(1)}, bf16[256,512]{0,1:T(8,128)(2,1)}, u32[]{:S(2)}, u32[]{:S(2)}) collective-permute-start(bf16[256,512]{0,1:T(8,128)(2,1)S(1)} %bitcast.88), channel_id=1, source_target_pairs={{0,16},{8,24},{16,32},{24,40},{32,48},{40,56},{48,64},{56,72},{64,... | collective-permute-start | bytes 786440 | tf_op jit(solution)/shard_map/ppermute | solution.py:15
  39.5 11.4 %collective-permute-start.7 = (bf16[256,512]{0,1:T(8,128)(2,1)S(1)}, bf16[256,512]{0,1:T(8,128)(2,1)}, u32[]{:S(2)}, u32[]{:S(2)}) collective-permute-start(bf16[256,512]{0,1:T(8,128)(2,1)S(1)} %bitcast.89), channel_id=1, source_target_pairs={{0,8},{8,16},{16,24},{24,32},{32,40},{40,48},{48,56},{56,64},{64,7... | collective-permute-start | bytes 786440 | tf_op jit(solution)/shard_map/ppermute | solution.py:15
  43.6 1.1 copy-start.11
  45.8 0.7 copy-start.10
  55.0 2.4 copy-start
  55.0 2.4 copy-start.1
  55.0 2.5 copy-start.6
  55.0 2.8 copy-start.5
  61.0 10.9 %copy-start.8 = (bf16[256,4,256]{2,0,1:T(8,128)(2,1)S(1)}, bf16[256,4,256]{2,0,1:T(8,128)(2,1)}, u32[]{:S(2)}) copy-start(bf16[256,4,256]{2,0,1:T(8,128)(2,1)} %copy.106) | copy-start | bytes 1572868
  83.6 5.4 %copy-start.4 = (f32[2,256,2,256]{3,1,2,0:T(8,128)S(1)}, f32[2,256,2,256]{3,1,2,0:T(8,128)}, u32[]{:S(2)}) copy-start(f32[2,256,2,256]{3,1,2,0:T(8,128)} %fusion.6) | copy-start | bytes 3145732
  89.0 2.7 copy-start.13
  96.0 12.3 %collective-permute-start.11 = (bf16[256,2,256]{0,2,1:T(8,128)(2,1)}, bf16[256,2,256]{0,2,1:T(8,128)(2,1)}, u32[]{:S(2)}, u32[]{:S(2)}) collective-permute-start(bf16[256,2,256]{0,2,1:T(8,128)(2,1)} %get-tuple-element.43), channel_id=1, source_target_pairs={{32,0},{40,8},{48,16},{56,24},{64,32},{72,40},{80,48},{88,56},{96,... | collective-permute-start | bytes 786440 | tf_op jit(solution)/shard_map/ppermute | solution.py:15
  97.3 13.3 %collective-permute-start.10 = (bf16[256,2,256]{0,2,1:T(8,128)(2,1)}, bf16[256,2,256]{0,2,1:T(8,128)(2,1)}, u32[]{:S(2)}, u32[]{:S(2)}) collective-permute-start(bf16[256,2,256]{0,2,1:T(8,128)(2,1)} %get-tuple-element.44), channel_id=1, source_target_pairs={{24,0},{32,8},{40,16},{48,24},{56,32},{64,40},{72,48},{80,56},{88,... | collective-permute-start | bytes 786440 | tf_op jit(solution)/shard_map/ppermute | solution.py:15
  98.6 24.7 %collective-permute-start.9 = (bf16[256,2,256]{0,2,1:T(8,128)(2,1)}, bf16[256,2,256]{0,2,1:T(8,128)(2,1)}, u32[]{:S(2)}, u32[]{:S(2)}) collective-permute-start(bf16[256,2,256]{0,2,1:T(8,128)(2,1)} %get-tuple-element.45), channel_id=1, source_target_pairs={{16,0},{24,8},{32,16},{40,24},{48,32},{56,40},{64,48},{72,56},{80,... | collective-permute-start | bytes 786440 | tf_op jit(solution)/shard_map/ppermute | solution.py:15
  99.9 32.3 %collective-permute-start.8 = (bf16[256,2,256]{0,2,1:T(8,128)(2,1)}, bf16[256,2,256]{0,2,1:T(8,128)(2,1)}, u32[]{:S(2)}, u32[]{:S(2)}) collective-permute-start(bf16[256,2,256]{0,2,1:T(8,128)(2,1)} %get-tuple-element.42), channel_id=1, source_target_pairs={{8,0},{16,8},{24,16},{32,24},{40,32},{48,40},{56,48},{64,56},{72,6... | collective-permute-start | bytes 786440 | tf_op jit(solution)/shard_map/ppermute | solution.py:15
  105.7 28.0 %copy-start.14 = (f32[256]{0:T(256)S(1)}, f32[256]{0:T(256)}, u32[]{:S(2)}) copy-start(f32[256]{0:T(256)} %param.11) | copy-start | bytes 3076
  107.0 28.0 %collective-permute-start.15 = (bf16[256,2,256]{0,2,1:T(8,128)(2,1)S(1)}, bf16[256,2,256]{0,2,1:T(8,128)(2,1)S(1)}, u32[]{:S(2)}, u32[]{:S(2)}) collective-permute-start(bf16[256,2,256]{0,2,1:T(8,128)(2,1)S(1)} %get-tuple-element.39), channel_id=1, source_target_pairs={{32,0},{40,8},{48,16},{56,24},{64,32},{72,40},{80,48},{88,56},{96,... | collective-permute-start | bytes 786440 | tf_op jit(solution)/shard_map/ppermute | solution.py:15
  108.3 26.7 %collective-permute-start.14 = (bf16[256,2,256]{0,2,1:T(8,128)(2,1)S(1)}, bf16[256,2,256]{0,2,1:T(8,128)(2,1)S(1)}, u32[]{:S(2)}, u32[]{:S(2)}) collective-permute-start(bf16[256,2,256]{0,2,1:T(8,128)(2,1)S(1)} %get-tuple-element.40), channel_id=1, source_target_pairs={{24,0},{32,8},{40,16},{48,24},{56,32},{64,40},{72,48},{80,56},{88,... | collective-permute-start | bytes 786440 | tf_op jit(solution)/shard_map/ppermute | solution.py:15
  110.6 29.5 %collective-permute-start.13 = (bf16[256,2,256]{0,2,1:T(8,128)(2,1)S(1)}, bf16[256,2,256]{0,2,1:T(8,128)(2,1)S(1)}, u32[]{:S(2)}, u32[]{:S(2)}) collective-permute-start(bf16[256,2,256]{0,2,1:T(8,128)(2,1)S(1)} %get-tuple-element.41), channel_id=1, source_target_pairs={{16,0},{24,8},{32,16},{40,24},{48,32},{56,40},{64,48},{72,56},{80,... | collective-permute-start | bytes 786440 | tf_op jit(solution)/shard_map/ppermute | solution.py:15
  123.3 18.6 %collective-permute-start.12 = (bf16[256,2,256]{0,2,1:T(8,128)(2,1)S(1)}, bf16[256,2,256]{0,2,1:T(8,128)(2,1)S(1)}, u32[]{:S(2)}, u32[]{:S(2)}) collective-permute-start(bf16[256,2,256]{0,2,1:T(8,128)(2,1)S(1)} %get-tuple-element.38), channel_id=1, source_target_pairs={{8,0},{16,8},{24,16},{32,24},{40,32},{48,40},{56,48},{64,56},{72,6... | collective-permute-start | bytes 786440 | tf_op jit(solution)/shard_map/ppermute | solution.py:15
  133.8 10.3 %copy-start.15 = (f32[256]{0:T(256)S(1)}, f32[256]{0:T(256)}, u32[]{:S(2)}) copy-start(f32[256]{0:T(256)} %get-tuple-element.30) | copy-start | bytes 3076
